TPU v7x, 128 devices: a whole 4x4x4 slice. The times are simulated.
128 devices in a mesh: vox: 8 (over y, core), fas: 16 (over z, x).
Axes of the slice: x: 4, y: 4, z: 4, core: 2. Of those that a mesh axis runs over, the one named last changes fastest.
Arguments:
- signal: float32 [128, 6144], P('vox', 'fas'), may hold values from -6 to 6
- initial_weights: float32 [524288], P('fas'), may hold values from 0.1 to 2
- coefficients: bfloat16 [32768, 4096], P(('vox', 'fas')), may hold values from 0 to 0.0234375
- block_rows: int32 [32768], P(('vox', 'fas')), may hold values from 0 to 127, as said below
- block_cols: int32 [32768], P(('vox', 'fas')), may hold values from 0 to 8191, as said below
- block_atoms: int32 [32768, 64], P(('vox', 'fas')), may hold values from 0 to 359
- block_count: int32 [128], P(('vox', 'fas')), may hold values from 64 to 256, as said below
- dictionary: bfloat16 [360, 96], replicated, may hold values from -6 to 6
Outputs:
- weights: float32 [524288], P('fas')
- residual: float32 [128, 6144], P('vox', 'fas')
Inputs may be any that keep to these rules, and one draw needn't show every extreme that they name: Block slots are stored device by device: the device with vox index i and fas index f holds slots (i * 16 + f) * 256 to (i * 16 + f + 1) * 256 - 1, and every block_rows value there lies in i * 16 to (i + 1) * 16 - 1. For the slots of the device with fas index f, every block_cols value lies in f * 512 to (f + 1) * 512 - 1. `block_count`: entry i * 16 + f is the number of live slots of the device with vox index i and fas index f, its first slots; some device has all 256 live.
All inputs are finite; a program needn't handle non-finite values.
Results may differ from a plain program's by a relative error of at most 0.0003.
Values sent between devices are 32-bit elements; how exact they have to be, the bound alone decides.
A program may use at most 128 MiB of HBM per device.

v0:
```python
import jax
import jax.numpy as jnp
from jax import lax
from jax.sharding import PartitionSpec as P

BV = 64
BF = 64
DIRS = 96
ITERS = 5


def local(
    signal,
    initial_weights,
    coefficients,
    block_rows,
    block_cols,
    block_atoms,
    block_count,
    dictionary,
):
    vox_rows = signal.shape[0]
    fas_rows = initial_weights.shape[0] // BF
    slot_total = coefficients.shape[0]
    row_width = BV * DIRS
    fas_place = lax.axis_index("fas")
    rows_local = block_rows - lax.axis_index("vox") * vox_rows
    cols_local = block_cols - fas_place * fas_rows
    live_count = block_count[0]
    atom_table = dictionary[block_atoms]
    coef_view = coefficients.reshape(slot_total, BV, BF)
    group_size = min(256, slot_total)
    group_turns = (live_count + group_size - 1) // group_size
    vox_range = jnp.arange(vox_rows, dtype=jnp.int32)
    fas_range = jnp.arange(fas_rows, dtype=jnp.int32)

    def group_pieces(first_slot):
        live_mask = (first_slot + jnp.arange(group_size, dtype=jnp.int32) < live_count).astype(
            jnp.float32
        )
        return (coef_view, atom_table, rows_local, cols_local, live_mask)

    def forward_partial(values):
        table = values.reshape(fas_rows, BF)

        def forward_accumulate(turn, running):
            coef_blk, atom_blk, rows_blk, cols_blk, live_mask = group_pieces(turn * group_size)
            scaled = coef_blk.astype(jnp.float32) * table[cols_blk][:, None, :]
            image_blk = jnp.einsum(
                "kvj,kjd->kvd",
                scaled,
                atom_blk.astype(jnp.float32),
                precision=lax.Precision.HIGHEST,
                preferred_element_type=jnp.float32,
            )
            selector = (rows_blk[:, None] == vox_range[None, :]).astype(jnp.float32) * live_mask[
                :, None
            ]
            added = jnp.dot(
                selector.T,
                image_blk.reshape(group_size, row_width),
                precision=lax.Precision.HIGHEST,
                preferred_element_type=jnp.float32,
            )
            return running + added

        start = jnp.zeros((vox_rows, row_width), jnp.float32)
        return lax.fori_loop(0, group_turns, forward_accumulate, start)

    def backward_partial(rows_view):

        def backward_accumulate(turn, running):
            coef_blk, atom_blk, rows_blk, cols_blk, live_mask = group_pieces(turn * group_size)
            gathered = rows_view[rows_blk]
            inner = jnp.einsum(
                "kvj,kvd->kjd",
                coef_blk.astype(jnp.float32),
                gathered,
                precision=lax.Precision.HIGHEST,
                preferred_element_type=jnp.float32,
            )
            contrib = jnp.sum(atom_blk.astype(jnp.float32) * inner, axis=-1)
            selector = (cols_blk[:, None] == fas_range[None, :]).astype(jnp.float32) * live_mask[
                :, None
            ]
            added = jnp.dot(
                selector.T,
                contrib,
                precision=lax.Precision.HIGHEST,
                preferred_element_type=jnp.float32,
            )
            return running + added

        start = jnp.zeros((fas_rows, BF), jnp.float32)
        running = lax.fori_loop(0, group_turns, backward_accumulate, start)
        return running.reshape(-1)

    def collect(partial_value):
        return lax.psum_scatter(partial_value, "fas", scatter_dimension=1, tiled=True)

    weights = initial_weights
    residual = collect(forward_partial(weights)) - signal
    for sweep in range(ITERS):
        whole_rows = lax.all_gather(residual, "fas", axis=1, tiled=True)
        gradient = lax.psum(backward_partial(whole_rows.reshape(vox_rows, BV, DIRS)), "vox")
        projected = jnp.where((weights > 0) | (gradient < 0), gradient, 0.0)
        image_pred = collect(forward_partial(projected))
        image_local = jnp.sum(image_pred * image_pred)
        grad_sq = lax.psum(jnp.sum(projected * projected), "fas")
        image_sq = lax.psum(image_local, ("vox", "fas"))
        step_size = grad_sq / (image_sq + 1e-06)
        weights = jnp.maximum(weights - step_size * projected, 0.0)
        residual = collect(forward_partial(weights)) - signal
    return (weights, residual)


def solution(mesh):
    placed = (
        P("vox", "fas"),
        P("fas"),
        P(("vox", "fas"), None),
        P(("vox", "fas")),
        P(("vox", "fas")),
        P(("vox", "fas"), None),
        P(("vox", "fas")),
        P(),
    )
    return jax.shard_map(
        local, mesh=mesh, in_specs=placed, out_specs=(P("fas"), P("vox", "fas")), check_vma=False
    )
```

profile of v0, /device:TPU:0, one launch (start us, length us, event | category | flops | bytes accessed | tf_op | source)
XLA Modules:
  0.0 2227.8 jit_solution(15539309578874618926)
XLA Ops:
  18.6 57.4 %gather_fusion = bf16[16384,96]{1,0:T(8,128)(2,1)} fusion(bf16[360,96]{1,0:T(8,128)(2,1)S(1)} %copy.28, s32[16384]{0:T(1024)S(1)} %broadcast_clamp_fusion), kind=kCustom, calls=%fused_computation | custom fusion | bytes 6356992 | tf_op jit(solution)/shard_map/gather | solution.py:30
  105.5 74.3 %reduce-scatter.12.cloned.1.call-done = f32[16,384]{1,0:T(8,128)} async-done(((f32[16,6144]{1,0:T(8,128)}), f32[16,384]{1,0:T(8,128)}) %reduce-scatter.12.cloned.1.call-update) | async-done | bytes 24592 | tf_op jit(solution)/shard_map/reduce_scatter | solution.py:99
  224.2 58.0 %all-reduce.6.cloned.1.call-done = f32[32768]{0:T(1024)} async-done(((f32[32768]{0:T(1024)}), f32[32768]{0:T(1024)}) %all-reduce.6.cloned.1.call-update) | async-done | bytes 131088 | tf_op jit(solution)/shard_map/psum | solution.py:105
  313.8 70.8 %reduce-scatter.14.cloned.1.call-done = f32[16,384]{1,0:T(8,128)} async-done(((f32[16,6144]{1,0:T(8,128)}), f32[16,384]{1,0:T(8,128)}) %reduce-scatter.14.cloned.1.call-update) | async-done | bytes 24592 | tf_op jit(solution)/shard_map/reduce_scatter | solution.py:99
  386.1 38.8 %psum.106 = f32[]{:T(128)} all-reduce(f32[]{:T(128)} %get-tuple-element.2460), channel_id=1, replica_groups=mesh['vox'=8,'fas'=16] {'fas'}, use_global_device_ids=true, to_apply=%region_8.9 | all-reduce | flops 1 | bytes 8 | tf_op jit(solution)/shard_map/psum | solution.py:109
  424.8 62.7 %psum.107 = f32[]{:T(128)} all-reduce(f32[]{:T(128)} %multiply_reduce_fusion.9), channel_id=1, replica_groups=mesh['vox'=8,'fas'=16] {'vox','fas'}, use_global_device_ids=true, to_apply=%region_13.14 | all-reduce | flops 1 | bytes 8 | tf_op jit(solution)/shard_map/psum | solution.py:110
  518.7 69.0 %reduce-scatter.16.cloned.1.call-done = f32[16,384]{1,0:T(8,128)} async-done(((f32[16,6144]{1,0:T(8,128)}), f32[16,384]{1,0:T(8,128)}) %reduce-scatter.16.cloned.1.call-update) | async-done | bytes 24592 | tf_op jit(solution)/shard_map/reduce_scatter | solution.py:99
  632.2 58.0 %all-reduce.8.cloned.1.call-done = f32[32768]{0:T(1024)} async-done(((f32[32768]{0:T(1024)}), f32[32768]{0:T(1024)}) %all-reduce.8.cloned.1.call-update) | async-done | bytes 131088 | tf_op jit(solution)/shard_map/psum | solution.py:105
  721.7 70.8 %reduce-scatter.18.cloned.1.call-done = f32[16,384]{1,0:T(8,128)} async-done(((f32[16,6144]{1,0:T(8,128)}), f32[16,384]{1,0:T(8,128)}) %reduce-scatter.18.cloned.1.call-update) | async-done | bytes 24592 | tf_op jit(solution)/shard_map/reduce_scatter | solution.py:99
  832.6 62.8 %psum.110 = f32[]{:T(128)} all-reduce(f32[]{:T(128)} %multiply_reduce_fusion.8), channel_id=1, replica_groups=mesh['vox'=8,'fas'=16] {'vox','fas'}, use_global_device_ids=true, to_apply=%region_27.28 | all-reduce | flops 1 | bytes 8 | tf_op jit(solution)/shard_map/psum | solution.py:110
  926.8 69.0 %reduce-scatter.20.cloned.1.call-done = f32[16,384]{1,0:T(8,128)} async-done(((f32[16,6144]{1,0:T(8,128)}), f32[16,384]{1,0:T(8,128)}) %reduce-scatter.20.cloned.1.call-update) | async-done | bytes 24592 | tf_op jit(solution)/shard_map/reduce_scatter | solution.py:99
  1040.3 58.0 %all-reduce.10.cloned.1.call-done = f32[32768]{0:T(1024)} async-done(((f32[32768]{0:T(1024)}), f32[32768]{0:T(1024)}) %all-reduce.10.cloned.1.call-update) | async-done | bytes 131088 | tf_op jit(solution)/shard_map/psum | solution.py:105
  1129.6 70.8 %reduce-scatter.22.cloned.1.call-done = f32[16,384]{1,0:T(8,128)} async-done(((f32[16,6144]{1,0:T(8,128)}), f32[16,384]{1,0:T(8,128)}) %reduce-scatter.22.cloned.1.call-update) | async-done | bytes 24592 | tf_op jit(solution)/shard_map/reduce_scatter | solution.py:99
  1201.9 38.8 %psum.112 = f32[]{:T(128)} all-reduce(f32[]{:T(128)} %get-tuple-element.2456), channel_id=1, replica_groups=mesh['vox'=8,'fas'=16] {'fas'}, use_global_device_ids=true, to_apply=%region_36.37 | all-reduce | flops 1 | bytes 8 | tf_op jit(solution)/shard_map/psum | solution.py:109
  1240.6 62.7 %psum.113 = f32[]{:T(128)} all-reduce(f32[]{:T(128)} %multiply_reduce_fusion.7), channel_id=1, replica_groups=mesh['vox'=8,'fas'=16] {'vox','fas'}, use_global_device_ids=true, to_apply=%region_41.42 | all-reduce | flops 1 | bytes 8 | tf_op jit(solution)/shard_map/psum | solution.py:110
  1334.7 69.1 %reduce-scatter.24.cloned.1.call-done = f32[16,384]{1,0:T(8,128)} async-done(((f32[16,6144]{1,0:T(8,128)}), f32[16,384]{1,0:T(8,128)}) %reduce-scatter.24.cloned.1.call-update) | async-done | bytes 24592 | tf_op jit(solution)/shard_map/reduce_scatter | solution.py:99
  1448.3 57.9 %all-reduce.12.cloned.1.call-done = f32[32768]{0:T(1024)} async-done(((f32[32768]{0:T(1024)}), f32[32768]{0:T(1024)}) %all-reduce.12.cloned.1.call-update) | async-done | bytes 131088 | tf_op jit(solution)/shard_map/psum | solution.py:105
  1537.6 70.8 %reduce-scatter.26.cloned.1.call-done = f32[16,384]{1,0:T(8,128)} async-done(((f32[16,6144]{1,0:T(8,128)}), f32[16,384]{1,0:T(8,128)}) %reduce-scatter.26.cloned.1.call-update) | async-done | bytes 24592 | tf_op jit(solution)/shard_map/reduce_scatter | solution.py:99
  1648.6 62.8 %psum.116 = f32[]{:T(128)} all-reduce(f32[]{:T(128)} %multiply_reduce_fusion.6), channel_id=1, replica_groups=mesh['vox'=8,'fas'=16] {'vox','fas'}, use_global_device_ids=true, to_apply=%region_55.56 | all-reduce | flops 1 | bytes 8 | tf_op jit(solution)/shard_map/psum | solution.py:110
  1742.7 69.0 %reduce-scatter.28.cloned.1.call-done = f32[16,384]{1,0:T(8,128)} async-done(((f32[16,6144]{1,0:T(8,128)}), f32[16,384]{1,0:T(8,128)}) %reduce-scatter.28.cloned.1.call-update) | async-done | bytes 24592 | tf_op jit(solution)/shard_map/reduce_scatter | solution.py:99
  1856.2 58.0 %all-reduce.14.cloned.1.call-done = f32[32768]{0:T(1024)} async-done(((f32[32768]{0:T(1024)}), f32[32768]{0:T(1024)}) %all-reduce.14.cloned.1.call-update) | async-done | bytes 131088 | tf_op jit(solution)/shard_map/psum | solution.py:105
  1945.5 70.8 %reduce-scatter.30.cloned.1.call-done = f32[16,384]{1,0:T(8,128)} async-done(((f32[16,6144]{1,0:T(8,128)}), f32[16,384]{1,0:T(8,128)}) %reduce-scatter.30.cloned.1.call-update) | async-done | bytes 24592 | tf_op jit(solution)/shard_map/reduce_scatter | solution.py:99
  2056.5 62.7 %psum.119 = f32[]{:T(128)} all-reduce(f32[]{:T(128)} %multiply_reduce_fusion.5), channel_id=1, replica_groups=mesh['vox'=8,'fas'=16] {'vox','fas'}, use_global_device_ids=true, to_apply=%region_69.70 | all-reduce | flops 1 | bytes 8 | tf_op jit(solution)/shard_map/psum | solution.py:110
  2150.5 69.0 %reduce-scatter.32.cloned.1.call-done = f32[16,384]{1,0:T(8,128)} async-done(((f32[16,6144]{1,0:T(8,128)}), f32[16,384]{1,0:T(8,128)}) %reduce-scatter.32.cloned.1.call-update) | async-done | bytes 24592 | tf_op jit(solution)/shard_map/reduce_scatter | solution.py:99
  (241 shorter events, 1006.3 us)
Async XLA Ops:
  7.2 10.8 copy-start.15
  7.2 11.1 copy-start.14
  7.2 11.2 copy-start.16
  7.2 11.2 copy-start.11
  7.2 172.5 %reduce-scatter.12.cloned.1.call-start = ((), (), s32[]{:S(2)}) async-start(), calls=%async_computation.11 | async-start | bytes 417792 | tf_op jit(solution)/shard_map/reduce_scatter | solution.py:99
  18.5 58.1 %copy-start.17 = (s32[256]{0:T(256)S(1)}, s32[256]{0:T(256)}, u32[]{:S(2)}) copy-start(s32[256]{0:T(256)} %param.43) | copy-start | bytes 3076
  76.7 103.0 %copy-start.12 = (f32[16,384]{1,0:T(8,128)S(1)}, f32[16,384]{1,0:T(8,128)}, u32[]{:S(2)}) copy-start(f32[16,384]{1,0:T(8,128)} %param.40) | copy-start | bytes 73732
  104.6 0.7 copy-start.1
  105.4 176.9 %all-reduce.6.cloned.1.call-start = ((), (), s32[]{:S(2)}) async-start(), calls=%async_computation.12 | async-start | bytes 262144 | tf_op jit(solution)/shard_map/psum | solution.py:105
  224.2 160.4 %reduce-scatter.14.cloned.1.call-start = ((), (), s32[]{:S(2)}) async-start(), calls=%async_computation.13 | async-start | bytes 417792 | tf_op jit(solution)/shard_map/reduce_scatter | solution.py:99
  313.8 274.0 %reduce-scatter.16.cloned.1.call-start = ((), (), s32[]{:S(2)}) async-start(), calls=%async_computation.14 | async-start | bytes 417792 | tf_op jit(solution)/shard_map/reduce_scatter | solution.py:99
  518.7 171.6 %all-reduce.8.cloned.1.call-start = ((), (), s32[]{:S(2)}) async-start(), calls=%async_computation.15 | async-start | bytes 262144 | tf_op jit(solution)/shard_map/psum | solution.py:105
  632.2 160.2 %reduce-scatter.18.cloned.1.call-start = ((), (), s32[]{:S(2)}) async-start(), calls=%async_computation.16 | async-start | bytes 417792 | tf_op jit(solution)/shard_map/reduce_scatter | solution.py:99
  721.6 274.2 %reduce-scatter.20.cloned.1.call-start = ((), (), s32[]{:S(2)}) async-start(), calls=%async_computation.17 | async-start | bytes 417792 | tf_op jit(solution)/shard_map/reduce_scatter | solution.py:99
  926.8 171.5 %all-reduce.10.cloned.1.call-start = ((), (), s32[]{:S(2)}) async-start(), calls=%async_computation.18 | async-start | bytes 262144 | tf_op jit(solution)/shard_map/psum | solution.py:105
  1040.2 160.2 %reduce-scatter.22.cloned.1.call-start = ((), (), s32[]{:S(2)}) async-start(), calls=%async_computation.19 | async-start | bytes 417792 | tf_op jit(solution)/shard_map/reduce_scatter | solution.py:99
  1129.6 274.2 %reduce-scatter.24.cloned.1.call-start = ((), (), s32[]{:S(2)}) async-start(), calls=%async_computation.20 | async-start | bytes 417792 | tf_op jit(solution)/shard_map/reduce_scatter | solution.py:99
  1334.7 171.5 %all-reduce.12.cloned.1.call-start = ((), (), s32[]{:S(2)}) async-start(), calls=%async_computation.21 | async-start | bytes 262144 | tf_op jit(solution)/shard_map/psum | solution.py:105
  1448.2 160.2 %reduce-scatter.26.cloned.1.call-start = ((), (), s32[]{:S(2)}) async-start(), calls=%async_computation.22 | async-start | bytes 417792 | tf_op jit(solution)/shard_map/reduce_scatter | solution.py:99
  1537.5 274.2 %reduce-scatter.28.cloned.1.call-start = ((), (), s32[]{:S(2)}) async-start(), calls=%async_computation.23 | async-start | bytes 417792 | tf_op jit(solution)/shard_map/reduce_scatter | solution.py:99
  1742.7 171.5 %all-reduce.14.cloned.1.call-start = ((), (), s32[]{:S(2)}) async-start(), calls=%async_computation.24 | async-start | bytes 262144 | tf_op jit(solution)/shard_map/psum | solution.py:105
  1856.1 160.2 %reduce-scatter.30.cloned.1.call-start = ((), (), s32[]{:S(2)}) async-start(), calls=%async_computation.25 | async-start | bytes 417792 | tf_op jit(solution)/shard_map/reduce_scatter | solution.py:99
  1945.5 274.0 %reduce-scatter.32.cloned.1.call-start = ((), (), s32[]{:S(2)}) async-start(), calls=%async_computation.26 | async-start | bytes 417792 | tf_op jit(solution)/shard_map/reduce_scatter | solution.py:99
  2120.6 0.9 copy-start.13
  (10 other events, 7.5 us)
Sparse Core Ops, SparseCore 0:
  105.5 74.1 reduce-scatter.11
  224.3 57.9 all-reduce.5
  313.9 70.6 reduce-scatter.13
  518.8 68.9 reduce-scatter.15
  632.3 57.8 all-reduce.7
  721.7 70.6 reduce-scatter.17
  926.9 68.9 reduce-scatter.19
  1040.4 57.8 all-reduce.9
  1129.7 70.6 reduce-scatter.21
  1334.8 68.9 reduce-scatter.23
  1448.3 57.8 all-reduce.11
  1537.7 70.6 reduce-scatter.25
  1742.8 68.9 reduce-scatter.27
  1856.3 57.8 all-reduce.13
  1945.6 70.6 reduce-scatter.29
  2150.6 68.8 reduce-scatter.31
where the time goes:
time: 2240 us; the launch traced here: 2230 us
  waiting for transfers between devices  1060 us (47%)
  blocking collectives  625 us (28%)
  matrix products  275 us (12%)
  local copies, waits for them, and re-layouts  207 us (9%)
  other arithmetic  30.5 us (1%)
  between operations  22.5 us (1%)
    reduce_scatter x11, waiting for transfers between devices, collect(): lax.psum_scatter(partial_value, 'fas', scatter_dimension=1, tiled=True)  773 us
    psum x5, blocking collectives, local(): image_sq = lax.psum(image_local, ('vox', 'fas'))  314 us
    psum x5, waiting for transfers between devices, local(): lax.psum(backward_partial(whole_rows.reshape(vox_rows, BV, DIRS)), 'vox')  290 us
    psum x5, blocking collectives, local(): grad_sq = lax.psum(jnp.sum(projected * projected), 'fas')  194 us
    dot_general x11, matrix products, forward_accumulate(): jnp.einsum('kvj,kjd->kvd', scaled, atom_blk.astype(jnp.float32), precisio...  124 us
    all_gather x5, blocking collectives, local(): whole_rows = lax.all_gather(residual, 'fas', axis=1, tiled=True)  118 us
    dot_general x11, local copies, waits for them, and re-layouts, forward_accumulate(): jnp.einsum('kvj,kjd->kvd', scaled, atom_blk.astype(jnp.float32), precisio...  94.4 us
    dot_general x11, matrix products, forward_accumulate(): jnp.dot(selector.T, image_blk.reshape(group_size, row_width), precision=l...  81.8 us
  transfers between devices with their start and end apart: 16, of which 16 were waited for; matrix products, arithmetic and copies ran while one was open for 0% of the time, Pallas kernels for 0%

commit v1 on v0

--- a/solution.py
+++ b/solution.py
@@ -101,7 +101,14 @@
     weights = initial_weights
     residual = collect(forward_partial(weights)) - signal
     for sweep in range(ITERS):
-        whole_rows = lax.all_gather(residual, "fas", axis=1, tiled=True)
+        ring = [residual]
+        for hop in range(15):
+            ring.append(lax.ppermute(ring[-1], "fas", [(dev, (dev + 1) % 16) for dev in range(16)]))
+        whole_rows = jnp.roll(
+            jnp.concatenate(ring[::-1], axis=1),
+            (lax.axis_index("fas") + 1) * ring[0].shape[1],
+            axis=1,
+        )
         gradient = lax.psum(backward_partial(whole_rows.reshape(vox_rows, BV, DIRS)), "vox")
         projected = jnp.where((weights > 0) | (gradient < 0), gradient, 0.0)
         image_pred = collect(forward_partial(projected))

time: 2240 us -> 2650 us (1.18)
  waiting for transfers between devices: 1060 us -> 1580 us
  blocking collectives: 625 us -> 507 us
    ppermute x0 -> x75, waiting for transfers between devices: none -> 530 us  [local(): lax.ppermute(ring[-1], 'fas', [(dev, (dev + 1) % 16) for dev in range(16)])]
    all_gather x5 -> x0, blocking collectives: 118 us -> none  [local(): whole_rows = lax.all_gather(residual, 'fas', axis=1, tiled=True)]
  transfers between devices with their start and end apart: 16 -> 91, of which waited for: 16 -> 91; matrix products, arithmetic and copies ran while one was open for 0% -> 0% of each run, Pallas kernels for 0% -> 0%
where the time goes in v1:
time: 2650 us; the launch traced here: 2640 us
  waiting for transfers between devices  1580 us (60%)
  blocking collectives  507 us (19%)
  matrix products  276 us (10%)
  local copies, waits for them, and re-layouts  209 us (8%)
  other arithmetic  32.1 us (1%)
    reduce_scatter x11, waiting for transfers between devices, collect(): lax.psum_scatter(partial_value, 'fas', scatter_dimension=1, tiled=True)  773 us
    ppermute x75, waiting for transfers between devices, local(): lax.ppermute(ring[-1], 'fas', [(dev, (dev + 1) % 16) for dev in range(16)])  530 us
    psum x5, blocking collectives, local(): image_sq = lax.psum(image_local, ('vox', 'fas'))  314 us
    psum x5, waiting for transfers between devices, local(): lax.psum(backward_partial(whole_rows.reshape(vox_rows, BV, DIRS)), 'vox')  278 us
    psum x5, blocking collectives, local(): grad_sq = lax.psum(jnp.sum(projected * projected), 'fas')  194 us
    dot_general x11, matrix products, forward_accumulate(): jnp.einsum('kvj,kjd->kvd', scaled, atom_blk.astype(jnp.float32), precisio...  124 us
    dot_general x11, local copies, waits for them, and re-layouts, forward_accumulate(): jnp.einsum('kvj,kjd->kvd', scaled, atom_blk.astype(jnp.float32), precisio...  94 us
    dot_general x11, matrix products, forward_accumulate(): jnp.dot(selector.T, image_blk.reshape(group_size, row_width), precision=l...  81.8 us
  transfers between devices with their start and end apart: 91, of which 91 were waited for; matrix products, arithmetic and copies ran while one was open for 0% of the time, Pallas kernels for 0%

profile of v1, /device:TPU:0, one launch (start us, length us, event | category | flops | bytes accessed | tf_op | source)
XLA Modules:
  0.0 2639.5 jit_solution(10455175167376392683)
XLA Ops:
  20.8 57.8 %gather_fusion = bf16[16384,96]{1,0:T(8,128)(2,1)} fusion(bf16[360,96]{1,0:T(8,128)(2,1)S(1)} %copy.28, s32[16384]{0:T(1024)S(1)} %broadcast_clamp_fusion), kind=kCustom, calls=%fused_computation | custom fusion | bytes 6356992 | tf_op jit(solution)/shard_map/gather | solution.py:30
  107.4 74.3 %reduce-scatter.12.cloned.1.call-done = f32[16,384]{1,0:T(8,128)} async-done(((f32[16,6144]{1,0:T(8,128)}), f32[16,384]{1,0:T(8,128)}) %reduce-scatter.12.cloned.1.call-update) | async-done | bytes 24592 | tf_op jit(solution)/shard_map/reduce_scatter | solution.py:99
  311.3 55.6 %all-reduce.6.cloned.1.call-done = f32[32768]{0:T(1024)} async-done(((f32[32768]{0:T(1024)}), f32[32768]{0:T(1024)}) %all-reduce.6.cloned.1.call-update) | async-done | bytes 131088 | tf_op jit(solution)/shard_map/psum | solution.py:112
  398.3 70.8 %reduce-scatter.14.cloned.1.call-done = f32[16,384]{1,0:T(8,128)} async-done(((f32[16,6144]{1,0:T(8,128)}), f32[16,384]{1,0:T(8,128)}) %reduce-scatter.14.cloned.1.call-update) | async-done | bytes 24592 | tf_op jit(solution)/shard_map/reduce_scatter | solution.py:99
  509.2 62.7 %psum.107 = f32[]{:T(128)} all-reduce(f32[]{:T(128)} %multiply_reduce_fusion.9), channel_id=1, replica_groups=mesh['vox'=8,'fas'=16] {'vox','fas'}, use_global_device_ids=true, to_apply=%region_13.15 | all-reduce | flops 1 | bytes 8 | tf_op jit(solution)/shard_map/psum | solution.py:117
  603.0 69.0 %reduce-scatter.16.cloned.1.call-done = f32[16,384]{1,0:T(8,128)} async-done(((f32[16,6144]{1,0:T(8,128)}), f32[16,384]{1,0:T(8,128)}) %reduce-scatter.16.cloned.1.call-update) | async-done | bytes 24592 | tf_op jit(solution)/shard_map/reduce_scatter | solution.py:99
  801.2 55.6 %all-reduce.8.cloned.1.call-done = f32[32768]{0:T(1024)} async-done(((f32[32768]{0:T(1024)}), f32[32768]{0:T(1024)}) %all-reduce.8.cloned.1.call-update) | async-done | bytes 131088 | tf_op jit(solution)/shard_map/psum | solution.py:112
  888.1 70.8 %reduce-scatter.18.cloned.1.call-done = f32[16,384]{1,0:T(8,128)} async-done(((f32[16,6144]{1,0:T(8,128)}), f32[16,384]{1,0:T(8,128)}) %reduce-scatter.18.cloned.1.call-update) | async-done | bytes 24592 | tf_op jit(solution)/shard_map/reduce_scatter | solution.py:99
  999.0 62.7 %psum.110 = f32[]{:T(128)} all-reduce(f32[]{:T(128)} %multiply_reduce_fusion.8), channel_id=1, replica_groups=mesh['vox'=8,'fas'=16] {'vox','fas'}, use_global_device_ids=true, to_apply=%region_27.29 | all-reduce | flops 1 | bytes 8 | tf_op jit(solution)/shard_map/psum | solution.py:117
  1092.8 69.0 %reduce-scatter.20.cloned.1.call-done = f32[16,384]{1,0:T(8,128)} async-done(((f32[16,6144]{1,0:T(8,128)}), f32[16,384]{1,0:T(8,128)}) %reduce-scatter.20.cloned.1.call-update) | async-done | bytes 24592 | tf_op jit(solution)/shard_map/reduce_scatter | solution.py:99
  1291.0 55.6 %all-reduce.10.cloned.1.call-done = f32[32768]{0:T(1024)} async-done(((f32[32768]{0:T(1024)}), f32[32768]{0:T(1024)}) %all-reduce.10.cloned.1.call-update) | async-done | bytes 131088 | tf_op jit(solution)/shard_map/psum | solution.py:112
  1377.9 70.8 %reduce-scatter.22.cloned.1.call-done = f32[16,384]{1,0:T(8,128)} async-done(((f32[16,6144]{1,0:T(8,128)}), f32[16,384]{1,0:T(8,128)}) %reduce-scatter.22.cloned.1.call-update) | async-done | bytes 24592 | tf_op jit(solution)/shard_map/reduce_scatter | solution.py:99
  1488.8 62.7 %psum.113 = f32[]{:T(128)} all-reduce(f32[]{:T(128)} %multiply_reduce_fusion.7), channel_id=1, replica_groups=mesh['vox'=8,'fas'=16] {'vox','fas'}, use_global_device_ids=true, to_apply=%region_41.43 | all-reduce | flops 1 | bytes 8 | tf_op jit(solution)/shard_map/psum | solution.py:117
  1582.6 69.0 %reduce-scatter.24.cloned.1.call-done = f32[16,384]{1,0:T(8,128)} async-done(((f32[16,6144]{1,0:T(8,128)}), f32[16,384]{1,0:T(8,128)}) %reduce-scatter.24.cloned.1.call-update) | async-done | bytes 24592 | tf_op jit(solution)/shard_map/reduce_scatter | solution.py:99
  1780.8 55.6 %all-reduce.12.cloned.1.call-done = f32[32768]{0:T(1024)} async-done(((f32[32768]{0:T(1024)}), f32[32768]{0:T(1024)}) %all-reduce.12.cloned.1.call-update) | async-done | bytes 131088 | tf_op jit(solution)/shard_map/psum | solution.py:112
  1867.8 70.8 %reduce-scatter.26.cloned.1.call-done = f32[16,384]{1,0:T(8,128)} async-done(((f32[16,6144]{1,0:T(8,128)}), f32[16,384]{1,0:T(8,128)}) %reduce-scatter.26.cloned.1.call-update) | async-done | bytes 24592 | tf_op jit(solution)/shard_map/reduce_scatter | solution.py:99
  1939.9 38.8 %psum.115 = f32[]{:T(128)} all-reduce(f32[]{:T(128)} %get-tuple-element.2455), channel_id=1, replica_groups=mesh['vox'=8,'fas'=16] {'fas'}, use_global_device_ids=true, to_apply=%region_50.52 | all-reduce | flops 1 | bytes 8 | tf_op jit(solution)/shard_map/psum | solution.py:116
  1978.7 62.7 %psum.116 = f32[]{:T(128)} all-reduce(f32[]{:T(128)} %multiply_reduce_fusion.6), channel_id=1, replica_groups=mesh['vox'=8,'fas'=16] {'vox','fas'}, use_global_device_ids=true, to_apply=%region_55.57 | all-reduce | flops 1 | bytes 8 | tf_op jit(solution)/shard_map/psum | solution.py:117
  2072.5 69.0 %reduce-scatter.28.cloned.1.call-done = f32[16,384]{1,0:T(8,128)} async-done(((f32[16,6144]{1,0:T(8,128)}), f32[16,384]{1,0:T(8,128)}) %reduce-scatter.28.cloned.1.call-update) | async-done | bytes 24592 | tf_op jit(solution)/shard_map/reduce_scatter | solution.py:99
  2270.6 55.6 %all-reduce.14.cloned.1.call-done = f32[32768]{0:T(1024)} async-done(((f32[32768]{0:T(1024)}), f32[32768]{0:T(1024)}) %all-reduce.14.cloned.1.call-update) | async-done | bytes 131088 | tf_op jit(solution)/shard_map/psum | solution.py:112
  2357.6 70.8 %reduce-scatter.30.cloned.1.call-done = f32[16,384]{1,0:T(8,128)} async-done(((f32[16,6144]{1,0:T(8,128)}), f32[16,384]{1,0:T(8,128)}) %reduce-scatter.30.cloned.1.call-update) | async-done | bytes 24592 | tf_op jit(solution)/shard_map/reduce_scatter | solution.py:99
  2429.7 38.8 %psum.118 = f32[]{:T(128)} all-reduce(f32[]{:T(128)} %get-tuple-element.2453), channel_id=1, replica_groups=mesh['vox'=8,'fas'=16] {'fas'}, use_global_device_ids=true, to_apply=%region_64.66 | all-reduce | flops 1 | bytes 8 | tf_op jit(solution)/shard_map/psum | solution.py:116
  2468.5 62.7 %psum.119 = f32[]{:T(128)} all-reduce(f32[]{:T(128)} %multiply_reduce_fusion.5), channel_id=1, replica_groups=mesh['vox'=8,'fas'=16] {'vox','fas'}, use_global_device_ids=true, to_apply=%region_69.71 | all-reduce | flops 1 | bytes 8 | tf_op jit(solution)/shard_map/psum | solution.py:117
  2562.3 69.1 %reduce-scatter.32.cloned.1.call-done = f32[16,384]{1,0:T(8,128)} async-done(((f32[16,6144]{1,0:T(8,128)}), f32[16,384]{1,0:T(8,128)}) %reduce-scatter.32.cloned.1.call-update) | async-done | bytes 24592 | tf_op jit(solution)/shard_map/reduce_scatter | solution.py:99
  (466 shorter events, 1429.9 us)
Async XLA Ops:
  7.2 174.5 %reduce-scatter.12.cloned.1.call-start = ((), (), s32[]{:S(2)}) async-start(), calls=%async_computation.11 | async-start | bytes 417792 | tf_op jit(solution)/shard_map/reduce_scatter | solution.py:99
  107.4 259.5 %all-reduce.6.cloned.1.call-start = ((), (), s32[]{:S(2)}) async-start(), calls=%async_computation.12 | async-start | bytes 262144 | tf_op jit(solution)/shard_map/psum | solution.py:112
  203.9 7.5 collective-permute-start.3
  282.8 7.7 collective-permute-start.14
  311.2 157.9 %reduce-scatter.14.cloned.1.call-start = ((), (), s32[]{:S(2)}) async-start(), calls=%async_computation.13 | async-start | bytes 417792 | tf_op jit(solution)/shard_map/reduce_scatter | solution.py:99
  398.2 273.8 %reduce-scatter.16.cloned.1.call-start = ((), (), s32[]{:S(2)}) async-start(), calls=%async_computation.14 | async-start | bytes 417792 | tf_op jit(solution)/shard_map/reduce_scatter | solution.py:99
  603.0 253.8 %all-reduce.8.cloned.1.call-start = ((), (), s32[]{:S(2)}) async-start(), calls=%async_computation.15 | async-start | bytes 262144 | tf_op jit(solution)/shard_map/psum | solution.py:112
  694.2 7.2 collective-permute-start.18
  744.3 7.5 collective-permute-start.25
  801.1 157.8 %reduce-scatter.18.cloned.1.call-start = ((), (), s32[]{:S(2)}) async-start(), calls=%async_computation.16 | async-start | bytes 417792 | tf_op jit(solution)/shard_map/reduce_scatter | solution.py:99
  888.1 273.8 %reduce-scatter.20.cloned.1.call-start = ((), (), s32[]{:S(2)}) async-start(), calls=%async_computation.17 | async-start | bytes 417792 | tf_op jit(solution)/shard_map/reduce_scatter | solution.py:99
  1092.8 253.8 %all-reduce.10.cloned.1.call-start = ((), (), s32[]{:S(2)}) async-start(), calls=%async_computation.18 | async-start | bytes 262144 | tf_op jit(solution)/shard_map/psum | solution.py:112
  1234.1 7.5 collective-permute-start.40
  1290.9 157.8 %reduce-scatter.22.cloned.1.call-start = ((), (), s32[]{:S(2)}) async-start(), calls=%async_computation.19 | async-start | bytes 417792 | tf_op jit(solution)/shard_map/reduce_scatter | solution.py:99
  1377.9 273.8 %reduce-scatter.24.cloned.1.call-start = ((), (), s32[]{:S(2)}) async-start(), calls=%async_computation.20 | async-start | bytes 417792 | tf_op jit(solution)/shard_map/reduce_scatter | solution.py:99
  1582.6 253.8 %all-reduce.12.cloned.1.call-start = ((), (), s32[]{:S(2)}) async-start(), calls=%async_computation.21 | async-start | bytes 262144 | tf_op jit(solution)/shard_map/psum | solution.py:112
  1673.8 7.2 collective-permute-start.48
  1723.9 7.5 collective-permute-start.55
  1780.7 157.8 %reduce-scatter.26.cloned.1.call-start = ((), (), s32[]{:S(2)}) async-start(), calls=%async_computation.22 | async-start | bytes 417792 | tf_op jit(solution)/shard_map/reduce_scatter | solution.py:99
  1867.7 273.8 %reduce-scatter.28.cloned.1.call-start = ((), (), s32[]{:S(2)}) async-start(), calls=%async_computation.23 | async-start | bytes 417792 | tf_op jit(solution)/shard_map/reduce_scatter | solution.py:99
  2072.4 253.8 %all-reduce.14.cloned.1.call-start = ((), (), s32[]{:S(2)}) async-start(), calls=%async_computation.24 | async-start | bytes 262144 | tf_op jit(solution)/shard_map/psum | solution.py:112
  2213.7 7.5 collective-permute-start.70
  2270.6 157.8 %reduce-scatter.30.cloned.1.call-start = ((), (), s32[]{:S(2)}) async-start(), calls=%async_computation.25 | async-start | bytes 417792 | tf_op jit(solution)/shard_map/reduce_scatter | solution.py:99
  2357.6 273.8 %reduce-scatter.32.cloned.1.call-start = ((), (), s32[]{:S(2)}) async-start(), calls=%async_computation.26 | async-start | bytes 417792 | tf_op jit(solution)/shard_map/reduce_scatter | solution.py:99
  (83 other events, 687.9 us)
Sparse Core Ops, SparseCore 0:
  107.5 74.1 reduce-scatter.11
  311.3 55.5 all-reduce.5
  398.3 70.6 reduce-scatter.13
  603.1 68.9 reduce-scatter.15
  801.3 55.4 all-reduce.7
  888.2 70.6 reduce-scatter.17
  1092.9 68.9 reduce-scatter.19
  1291.0 55.4 all-reduce.9
  1378.0 70.6 reduce-scatter.21
  1582.7 68.9 reduce-scatter.23
  1780.9 55.4 all-reduce.11
  1867.8 70.6 reduce-scatter.25
  2072.6 68.9 reduce-scatter.27
  2270.7 55.5 all-reduce.13
  2357.7 70.6 reduce-scatter.29
  2562.4 68.9 reduce-scatter.31
